TPU v7x, 32 devices: a whole 2x2x4 slice. The times are simulated.
32 devices in a mesh: ens: 2 (over y), row: 4 (over z), col: 4 (over x, core).
Axes of the slice: x: 2, y: 2, z: 4, core: 2. Of those that a mesh axis runs over, the one named last changes fastest.
Arguments:
- series: float32 [24576, 256], P(('ens', 'row', 'col')), parts along dimension 0, may hold values from -22 to 22, as said below
- vectors: float32 [24576, 128], P(('ens', 'row', 'col')), parts along dimension 0, may hold values from -6 to 6
- damp_class: int32 [24576], P(('ens', 'row', 'col')), parts along dimension 0, may hold values from 0 to 15
- damp_levels: float32 [16], replicated, may hold values from 0.5 to 2
- removed_blocks: int32 [64, 32], P('ens'), parts along dimension 0, may hold values 0 or 1
Outputs:
- filtered: float32 [24576, 128], P(('ens', 'row', 'col')), parts along dimension 0
There are 2 independent parts, one for each index of `ens`. A program takes and returns all parts, laid end to end along the dimension named above; an argument that names none is the same for every part. Nothing has to cross between parts.
Inputs may be any that keep to these rules, and one draw needn't show every extreme that they name: Each voxel's series is not constant.
All inputs are finite; a program needn't handle non-finite values.
Results may differ from a plain program's by a relative error of at most 0.0003.
Values sent between devices are 32-bit elements; how exact they have to be, the bound alone decides.
No kernel may reach another device: no remote copies, remote signals or barrier semaphores. Data moves between devices by JAX's collectives and lax.ppermute only.
A program may use at most 128 MiB of HBM per device.

v0:
```python
import jax
import jax.numpy as jnp
from jax import lax
from jax.sharding import PartitionSpec as P

N = 12288
sharpness = 12.0


def standardize(series):
    centered = series - jnp.mean(series, axis=1, keepdims=True)
    spread = jnp.mean(centered * centered, axis=1, keepdims=True)
    return centered * lax.rsqrt(spread + 1e-05)


def local(series, vectors, damp_class, damp_levels, removed_blocks):
    n_col = lax.axis_size("col")
    row_id = lax.axis_index("row")
    col_id = lax.axis_index("col")
    shard_rows = series.shape[0]
    samples = series.shape[1]
    classes = damp_levels.shape[0]
    z_own = standardize(series)
    onehot = (damp_class[:, None] == jnp.arange(classes, dtype=jnp.int32)[None, :]).astype(
        jnp.float32
    )
    damping = jnp.sum(onehot * damp_levels[None, :], axis=1)
    z_rows, d_rows = (
        lax.all_gather(z_own, "col", axis=0, tiled=True),
        lax.all_gather(damping, "col", axis=0, tiled=True),
    )
    tile_rows = z_rows.shape[0]
    blocks = removed_blocks.shape[0]
    block_size = N // blocks
    row_blocks = tile_rows // block_size
    keep_rows = 1.0 - lax.dynamic_slice_in_dim(
        removed_blocks, row_id * row_blocks, row_blocks, 0
    ).astype(jnp.float32)
    shard_piece = lax.all_gather(z_own, "row", axis=0, tiled=True)
    count = shard_piece.shape[0]
    position = jnp.arange(count, dtype=jnp.int32)
    owner_row = position // shard_rows
    global_index = (owner_row * n_col + col_id) * shard_rows + position % shard_rows
    col_block = global_index // block_size
    onehot_cols = (col_block[None, :] == jnp.arange(blocks, dtype=jnp.int32)[:, None]).astype(
        jnp.float32
    )
    keep_small = jnp.dot(
        keep_rows, onehot_cols, precision=lax.Precision.HIGHEST, preferred_element_type=jnp.float32
    )
    keep_full = jnp.broadcast_to(keep_small[:, None, :], (row_blocks, block_size, count)).reshape(
        tile_rows, count
    )
    correlation = (
        lax.dot_general(
            z_rows,
            shard_piece,
            (((1,), (1,)), ((), ())),
            precision=lax.Precision.HIGHEST,
            preferred_element_type=jnp.float32,
        )
        / samples
    )
    affinity = jnp.tanh(sharpness * correlation) * keep_full * d_rows[:, None]
    spectral_scale = 0.5 * N * jnp.mean(damp_levels * damp_levels)

    def forward_add(shard_piece):
        return jnp.dot(
            affinity,
            shard_piece,
            precision=lax.Precision.HIGHEST,
            preferred_element_type=jnp.float32,
        )

    def backward_add(shard_piece):
        return lax.dot_general(
            affinity,
            shard_piece,
            (((0,), (0,)), ((), ())),
            precision=lax.Precision.HIGHEST,
            preferred_element_type=jnp.float32,
        )

    def normal_apply(field_in):
        product = forward_add(lax.all_gather(field_in, "row", axis=0, tiled=True))
        product = lax.psum_scatter(product, "col", scatter_dimension=0, tiled=True)
        returned = backward_add(lax.all_gather(product, "col", axis=0, tiled=True))
        return lax.psum_scatter(returned, "row", scatter_dimension=0, tiled=True) / spectral_scale

    first_term = normal_apply(vectors) - vectors
    filtered = 2.0 * (normal_apply(first_term) - first_term) - vectors
    return filtered


def solution(mesh):
    placed = (
        P(("ens", "row", "col"), None),
        P(("ens", "row", "col"), None),
        P(("ens", "row", "col")),
        P(),
        P("ens", None),
    )
    return jax.shard_map(
        local, mesh=mesh, in_specs=placed, out_specs=P(("ens", "row", "col"), None), check_vma=False
    )
```

profile of v0, /device:TPU:0, one launch (start us, length us, event | category | flops | bytes accessed | tf_op | source)
XLA Modules:
  0.0 560.3 jit_solution(4432875654553335063)
XLA Ops:
  6.5 1.3 reduce_sum.36
  7.9 1.4 multiply_reduce_fusion
  9.3 2.3 subtract_multiply_fusion
  11.7 0.7 all-gather.8.cloned.1.call-update
  12.4 0.7 all-gather.12.cloned.1.call-update
  13.3 6.2 %all-gather = f32[4,1,768]{2,1,0:T(1,128)S(1)} all-gather(f32[1,1,768]{2,1,0:T(1,128)S(1)} %reshape.49), channel_id=1, replica_groups=mesh['ens'=2,'row'=4,'col'=4] {'col'}, dimensions={0}, use_global_device_ids=true | all-gather | bytes 15360 | tf_op jit(solution)/shard_map/all_gather | solution.py:30
  19.5 0.9 fusion.1
  20.5 57.5 %all-gather.10.cloned.1.call-done = f32[3072,256]{1,0:T(8,128)} async-done(((f32[768,256]{1,0:T(8,128)}), f32[3072,256]{1,0:T(8,128)}) %all-gather.10.cloned.1.call-update) | async-done | bytes 3145744 | tf_op jit(solution)/shard_map/all_gather | solution.py:39
  78.0 28.7 %all-gather.8.cloned.1.call-done = f32[3072,256]{1,0:T(8,128)} async-done(((f32[768,256]{1,0:T(8,128)}), f32[3072,256]{1,0:T(8,128)}) %all-gather.8.cloned.1.call-update) | async-done | bytes 3145744 | tf_op jit(solution)/shard_map/all_gather | solution.py:29
  106.7 40.0 %fusion = f32[3072,3072]{1,0:T(8,128)} fusion(f32[3072,256]{1,0:T(8,128)} %all-gather.8.cloned.1.call-done, f32[3072,256]{1,0:T(8,128)} %all-gather.10.cloned.1.call-done, f32[3072]{0:T(1024)S(1)} %bitcast.15, f32[8,3072]{1,0:T(8,128)S(1)} %fusion.1), kind=kOutput, calls=%fused_computation.1 | convolution fusion | flops 29019340800 | bytes 44150784 | tf_op jit(solution)/shard_map/dot_general | solution.py:55
  146.7 34.9 %fusion.21 = f32[3072,128]{1,0:T(8,128)} fusion(f32[3072,3072]{1,0:T(8,128)} %fusion, f32[3072,128]{1,0:T(8,128)} %all-gather.12.cloned.1.call-done), kind=kOutput, calls=%fused_computation.39 | convolution fusion | flops 14495514624 | bytes 40894464 | tf_op jit(solution)/shard_map/dot_general | solution.py:68
  181.7 28.1 %reduce-scatter.5.cloned.1.call-done = f32[768,128]{1,0:T(8,128)} async-done(((f32[3072,128]{1,0:T(8,128)}), f32[768,128]{1,0:T(8,128)}) %reduce-scatter.5.cloned.1.call-update) | async-done | bytes 393232 | tf_op jit(solution)/shard_map/reduce_scatter | solution.py:86
  209.9 21.0 %all-gather.14.cloned.1.call-done = f32[3072,128]{1,0:T(8,128)} async-done(((f32[768,128]{1,0:T(8,128)}), f32[3072,128]{1,0:T(8,128)}) %all-gather.14.cloned.1.call-update) | async-done | bytes 1572880 | tf_op jit(solution)/shard_map/all_gather | solution.py:87
  230.9 64.5 %fusion.22 = f32[3072,128]{1,0:T(8,128)} fusion(f32[3072,3072]{1,0:T(8,128)} %fusion, f32[3072,128]{1,0:T(8,128)} %all-gather.14.cloned.1.call-done), kind=kOutput, calls=%fused_computation.40 | convolution fusion | flops 14495514624 | bytes 40894464 | tf_op jit(solution)/shard_map/dot_general | solution.py:76
  295.5 0.6 multiply_reduce_fusion.1
  296.7 34.3 %reduce-scatter.7.cloned.1.call-done = f32[768,128]{1,0:T(8,128)} async-done(((f32[3072,128]{1,0:T(8,128)}), f32[768,128]{1,0:T(8,128)}) %reduce-scatter.7.cloned.1.call-update) | async-done | bytes 393232 | tf_op jit(solution)/shard_map/reduce_scatter | solution.py:88
  331.0 1.8 divide_subtract_fusion
  332.9 36.0 %all-gather.16.cloned.1.call-done = f32[3072,128]{1,0:T(8,128)} async-done(((f32[768,128]{1,0:T(8,128)}), f32[3072,128]{1,0:T(8,128)}) %all-gather.16.cloned.1.call-update) | async-done | bytes 1572880 | tf_op jit(solution)/shard_map/all_gather | solution.py:85
  368.8 34.7 %fusion.23 = f32[3072,128]{1,0:T(8,128)} fusion(f32[3072,3072]{1,0:T(8,128)} %fusion, f32[3072,128]{1,0:T(8,128)} %all-gather.16.cloned.1.call-done), kind=kOutput, calls=%fused_computation.41 | convolution fusion | flops 14495514624 | bytes 40894464 | tf_op jit(solution)/shard_map/dot_general | solution.py:68
  403.6 27.0 %reduce-scatter.9.cloned.1.call-done = f32[768,128]{1,0:T(8,128)} async-done(((f32[3072,128]{1,0:T(8,128)}), f32[768,128]{1,0:T(8,128)}) %reduce-scatter.9.cloned.1.call-update) | async-done | bytes 393232 | tf_op jit(solution)/shard_map/reduce_scatter | solution.py:86
  430.7 21.1 %all-gather.18.cloned.1.call-done = f32[3072,128]{1,0:T(8,128)} async-done(((f32[768,128]{1,0:T(8,128)}), f32[3072,128]{1,0:T(8,128)}) %all-gather.18.cloned.1.call-update) | async-done | bytes 1572880 | tf_op jit(solution)/shard_map/all_gather | solution.py:87
  451.8 64.0 %fusion.24 = f32[3072,128]{1,0:T(8,128)} fusion(f32[3072,3072]{1,0:T(8,128)} %fusion, f32[3072,128]{1,0:T(8,128)} %all-gather.18.cloned.1.call-done), kind=kOutput, calls=%fused_computation.42 | convolution fusion | flops 14495514624 | bytes 40894464 | tf_op jit(solution)/shard_map/dot_general | solution.py:76
  515.9 35.6 %reduce-scatter.11.cloned.1.call-done = f32[768,128]{1,0:T(8,128)} async-done(((f32[3072,128]{1,0:T(8,128)}), f32[768,128]{1,0:T(8,128)}) %reduce-scatter.11.cloned.1.call-update) | async-done | bytes 393232 | tf_op jit(solution)/shard_map/reduce_scatter | solution.py:88
  551.5 1.8 multiply_subtract_fusion
  (32 shorter events, 0.6 us)
Async XLA Ops:
  6.5 6.6 %copy-start.2 = (s32[768]{0:T(1024)S(1)}, s32[768]{0:T(1024)}, u32[]{:S(2)}) copy-start(s32[768]{0:T(1024)} %param.7) | copy-start | bytes 9220
  6.5 6.7 %copy-start.3 = (f32[16]{0:T(128)S(1)}, f32[16]{0:T(128)}, u32[]{:S(2)}) copy-start(f32[16]{0:T(128)} %param.8) | copy-start | bytes 196
  6.5 71.4 %all-gather.10.cloned.1.call-start = ((), (), s32[]{:S(2)}) async-start(), calls=%async_computation.5 | async-start | bytes 3932160 | tf_op jit(solution)/shard_map/all_gather | solution.py:39
  11.6 95.1 %all-gather.8.cloned.1.call-start = ((), (), s32[]{:S(2)}) async-start(), calls=%async_computation.4 | async-start | bytes 3932160 | tf_op jit(solution)/shard_map/all_gather | solution.py:29
  12.4 134.3 %all-gather.12.cloned.1.call-start = ((), (), s32[]{:S(2)}) async-start(), calls=%async_computation.6 | async-start | bytes 1966080 | tf_op jit(solution)/shard_map/all_gather | solution.py:85
  13.1 196.7 %reduce-scatter.5.cloned.1.call-start = ((), (), s32[]{:S(2)}) async-start(), calls=%async_computation.7 | async-start | bytes 1966080 | tf_op jit(solution)/shard_map/reduce_scatter | solution.py:86
  181.6 49.3 %all-gather.14.cloned.1.call-start = ((), (), s32[]{:S(2)}) async-start(), calls=%async_computation.8 | async-start | bytes 1966080 | tf_op jit(solution)/shard_map/all_gather | solution.py:87
  209.8 121.2 %copy-start = (f32[768,128]{1,0:T(8,128)S(1)}, f32[768,128]{1,0:T(8,128)}, u32[]{:S(2)}) copy-start(f32[768,128]{1,0:T(8,128)} %param.6) | copy-start | bytes 1179652
  209.8 121.2 %reduce-scatter.7.cloned.1.call-start = ((), (), s32[]{:S(2)}) async-start(), calls=%async_computation.9 | async-start | bytes 1966080 | tf_op jit(solution)/shard_map/reduce_scatter | solution.py:88
  295.4 73.4 %all-gather.16.cloned.1.call-start = ((), (), s32[]{:S(2)}) async-start(), calls=%async_computation.10 | async-start | bytes 1966080 | tf_op jit(solution)/shard_map/all_gather | solution.py:85
  332.8 97.8 %reduce-scatter.9.cloned.1.call-start = ((), (), s32[]{:S(2)}) async-start(), calls=%async_computation.11 | async-start | bytes 1966080 | tf_op jit(solution)/shard_map/reduce_scatter | solution.py:86
  403.6 48.2 %all-gather.18.cloned.1.call-start = ((), (), s32[]{:S(2)}) async-start(), calls=%async_computation.12 | async-start | bytes 1966080 | tf_op jit(solution)/shard_map/all_gather | solution.py:87
  430.6 120.8 %copy-start.1 = (f32[768,128]{1,0:T(8,128)S(1)}, f32[768,128]{1,0:T(8,128)}, u32[]{:S(2)}) copy-start(f32[768,128]{1,0:T(8,128)} %reduce-scatter.7.cloned.1.call-done) | copy-start | bytes 1179652
  430.6 120.8 %reduce-scatter.11.cloned.1.call-start = ((), (), s32[]{:S(2)}) async-start(), calls=%async_computation.13 | async-start | bytes 1966080 | tf_op jit(solution)/shard_map/reduce_scatter | solution.py:88
Sparse Core Ops, SparseCore 0:
  11.8 66.1 all-gather.9
  79.5 27.1 all-gather.7
  108.3 37.0 all-gather.11
  181.7 28.0 reduce-scatter.4
  211.2 19.6 all-gather.13
  295.5 35.4 reduce-scatter.6
  332.9 35.8 all-gather.15
  403.7 26.8 reduce-scatter.8
  432.2 19.6 all-gather.17
  516.0 35.4 reduce-scatter.10
where the time goes:
time: 568 us; the launch traced here: 560 us
  waiting for transfers between devices  291 us (51%)
  matrix products  239 us (42%)
  between operations  14.5 us (3%)
  other arithmetic  9.36 us (2%)
  blocking collectives  6.21 us (1%)
    dot_general x2, matrix products, backward_add(): lax.dot_general(affinity, shard_piece, (((0,), (0,)), ((), ())), precisio...  129 us
    reduce_scatter x2, waiting for transfers between devices, normal_apply(): lax.psum_scatter(returned, 'row', scatter_dimension=0, tiled=True)  69.9 us
    dot_general x2, matrix products, forward_add(): jnp.dot(affinity, shard_piece, precision=lax.Precision.HIGHEST, preferred...  69.6 us
    all_gather x1, waiting for transfers between devices, local(): shard_piece = lax.all_gather(z_own, 'row', axis=0, tiled=True)  57.5 us
    reduce_scatter x2, waiting for transfers between devices, normal_apply(): product = lax.psum_scatter(product, 'col', scatter_dimension=0, tiled=True)  55.1 us
    all_gather x2, waiting for transfers between devices, normal_apply(): returned = backward_add(lax.all_gather(product, 'col', axis=0, tiled=True))  42.1 us
    dot_general x1, matrix products, local(): lax.dot_general(z_rows, shard_piece, (((1,), (1,)), ((), ())), precision=...  40 us
    all_gather x2, waiting for transfers between devices, normal_apply(): product = forward_add(lax.all_gather(field_in, 'row', axis=0, tiled=True))  36 us
  transfers between devices with their start and end apart: 10, of which 9 were waited for; matrix products, arithmetic and copies ran while one was open for 7% of the time, Pallas kernels for 0%

commit v1 on v0

--- a/solution.py
+++ b/solution.py
@@ -5,6 +5,21 @@
 
 N = 12288
 sharpness = 12.0
+
+
+def replace_pools(row_data, d_out):
+    mesh_name = "row"
+    n_lanes = lax.axis_size(mesh_name)
+    y_new = row_data
+    chunks = [y_new]
+    j = 0
+    now = [(kk - 1, kk) for kk in range(1, n_lanes)] + [(n_lanes - 1, 0)]
+    while j < n_lanes - 1:
+        y_new = lax.ppermute(y_new, mesh_name, now)
+        chunks += [y_new]
+        j += 1
+    last = jnp.concatenate([*reversed(chunks)], axis=d_out)
+    return jnp.roll(last, shift=(lax.axis_index(mesh_name) + 1) * y_new.shape[d_out], axis=d_out)
 
 
 def standardize(series):
@@ -36,7 +51,7 @@
     keep_rows = 1.0 - lax.dynamic_slice_in_dim(
         removed_blocks, row_id * row_blocks, row_blocks, 0
     ).astype(jnp.float32)
-    shard_piece = lax.all_gather(z_own, "row", axis=0, tiled=True)
+    shard_piece = replace_pools(z_own, 0)
     count = shard_piece.shape[0]
     position = jnp.arange(count, dtype=jnp.int32)
     owner_row = position // shard_rows

time: 568 us -> 547 us (0.963)
  waiting for transfers between devices: 291 us -> 265 us
    ppermute x0 -> x3, waiting for transfers between devices: none -> 61.6 us  [replace_pools(): y_new = lax.ppermute(y_new, mesh_name, now)]
    all_gather x1 -> x0, waiting for transfers between devices: 57.5 us -> none  [local(): shard_piece = lax.all_gather(z_own, 'row', axis=0, tiled=True)]
    all_gather x1, waiting for transfers between devices: 28.7 us -> 0.02 us  [local(): lax.all_gather(z_own, 'col', axis=0, tiled=True)]
  transfers between devices with their start and end apart: 10 -> 12, of which waited for: 9 -> 10; matrix products, arithmetic and copies ran while one was open for 7% -> 8% of each run, Pallas kernels for 0% -> 0%
where the time goes in v1:
time: 547 us; the launch traced here: 538 us
  waiting for transfers between devices  265 us (48%)
  matrix products  239 us (44%)
  between operations  14.3 us (3%)
  other arithmetic  10.7 us (2%)
    dot_general x2, matrix products, backward_add(): lax.dot_general(affinity, shard_piece, (((0,), (0,)), ((), ())), precisio...  129 us
    reduce_scatter x2, waiting for transfers between devices, normal_apply(): lax.psum_scatter(returned, 'row', scatter_dimension=0, tiled=True)  69.9 us
    dot_general x2, matrix products, forward_add(): jnp.dot(affinity, shard_piece, precision=lax.Precision.HIGHEST, preferred...  69.6 us
    ppermute x3, waiting for transfers between devices, replace_pools(): y_new = lax.ppermute(y_new, mesh_name, now)  61.6 us
    reduce_scatter x2, waiting for transfers between devices, normal_apply(): product = lax.psum_scatter(product, 'col', scatter_dimension=0, tiled=True)  55.5 us
    all_gather x2, waiting for transfers between devices, normal_apply(): returned = backward_add(lax.all_gather(product, 'col', axis=0, tiled=True))  42.2 us
    dot_general x1, matrix products, local(): lax.dot_general(z_rows, shard_piece, (((1,), (1,)), ((), ())), precision=...  39.9 us
    all_gather x2, waiting for transfers between devices, normal_apply(): product = forward_add(lax.all_gather(field_in, 'row', axis=0, tiled=True))  36 us
  transfers between devices with their start and end apart: 12, of which 10 were waited for; matrix products, arithmetic and copies ran while one was open for 8% of the time, Pallas kernels for 0%

profile of v1, /device:TPU:0, one launch (start us, length us, event | category | flops | bytes accessed | tf_op | source)
XLA Modules:
  0.0 538.2 jit_solution(14721913795259209321)
XLA Ops:
  6.5 1.4 reduce_sum.36
  7.9 1.4 multiply_reduce_fusion
  9.4 2.3 subtract_multiply_fusion
  11.7 3.1 collective-permute-start
  14.8 19.8 %collective-permute-done = f32[768,256]{1,0:T(8,128)S(1)} collective-permute-done((f32[768,256]{1,0:T(8,128)}, f32[768,256]{1,0:T(8,128)S(1)}, u32[]{:S(2)}, u32[]{:S(2)}) %collective-permute-start) | collective-permute-done | bytes 786464 | tf_op jit(solution)/shard_map/ppermute | solution.py:18
  34.6 20.5 %collective-permute-done.1 = f32[768,256]{1,0:T(8,128)S(1)} collective-permute-done((f32[768,256]{1,0:T(8,128)S(1)}, f32[768,256]{1,0:T(8,128)S(1)}, u32[]{:S(2)}, u32[]{:S(2)}) %collective-permute-start.1) | collective-permute-done | bytes 786464 | tf_op jit(solution)/shard_map/ppermute | solution.py:18
  55.2 0.8 select_reduce_fusion
  56.0 5.2 all-gather
  61.2 0.9 fusion.2
  62.2 21.3 %collective-permute-done.2 = f32[768,256]{1,0:T(8,128)S(1)} collective-permute-done((f32[768,256]{1,0:T(8,128)S(1)}, f32[768,256]{1,0:T(8,128)S(1)}, u32[]{:S(2)}, u32[]{:S(2)}) %collective-permute-start.2) | collective-permute-done | bytes 786464 | tf_op jit(solution)/shard_map/ppermute | solution.py:18
  84.7 39.9 %fusion = f32[3072,3072]{1,0:T(8,128)} fusion(f32[3072,256]{1,0:T(8,128)} %all-gather.7.cloned.1.call-done, f32[3072]{0:T(1024)S(1)} %bitcast.17, f32[8,3072]{1,0:T(8,128)S(1)} %fusion.2, f32[3072,256]{1,0:T(8,128)S(1)} %fusion.39), kind=kOutput, calls=%fused_computation.1 | convolution fusion | flops 29019340800 | bytes 44150784 | tf_op jit(solution)/shard_map/dot_general | solution.py:70
  124.5 34.9 %fusion.23 = f32[3072,128]{1,0:T(8,128)} fusion(f32[3072,3072]{1,0:T(8,128)} %fusion, f32[3072,128]{1,0:T(8,128)} %all-gather.9.cloned.1.call-done), kind=kOutput, calls=%fused_computation.49 | convolution fusion | flops 14495514624 | bytes 40894464 | tf_op jit(solution)/shard_map/dot_general | solution.py:83
  159.5 28.5 %reduce-scatter.5.cloned.1.call-done = f32[768,128]{1,0:T(8,128)} async-done(((f32[3072,128]{1,0:T(8,128)}), f32[768,128]{1,0:T(8,128)}) %reduce-scatter.5.cloned.1.call-update) | async-done | bytes 393232 | tf_op jit(solution)/shard_map/reduce_scatter | solution.py:101
  188.1 21.0 %all-gather.11.cloned.1.call-done = f32[3072,128]{1,0:T(8,128)} async-done(((f32[768,128]{1,0:T(8,128)}), f32[3072,128]{1,0:T(8,128)}) %all-gather.11.cloned.1.call-update) | async-done | bytes 1572880 | tf_op jit(solution)/shard_map/all_gather | solution.py:102
  209.1 64.5 %fusion.24 = f32[3072,128]{1,0:T(8,128)} fusion(f32[3072,3072]{1,0:T(8,128)} %fusion, f32[3072,128]{1,0:T(8,128)} %all-gather.11.cloned.1.call-done), kind=kOutput, calls=%fused_computation.50 | convolution fusion | flops 14495514624 | bytes 40894464 | tf_op jit(solution)/shard_map/dot_general | solution.py:91
  274.9 34.3 %reduce-scatter.7.cloned.1.call-done = f32[768,128]{1,0:T(8,128)} async-done(((f32[3072,128]{1,0:T(8,128)}), f32[768,128]{1,0:T(8,128)}) %reduce-scatter.7.cloned.1.call-update) | async-done | bytes 393232 | tf_op jit(solution)/shard_map/reduce_scatter | solution.py:103
  309.2 1.8 divide_subtract_fusion
  311.0 36.0 %all-gather.13.cloned.1.call-done = f32[3072,128]{1,0:T(8,128)} async-done(((f32[768,128]{1,0:T(8,128)}), f32[3072,128]{1,0:T(8,128)}) %all-gather.13.cloned.1.call-update) | async-done | bytes 1572880 | tf_op jit(solution)/shard_map/all_gather | solution.py:100
  347.0 34.7 %fusion.25 = f32[3072,128]{1,0:T(8,128)} fusion(f32[3072,3072]{1,0:T(8,128)} %fusion, f32[3072,128]{1,0:T(8,128)} %all-gather.13.cloned.1.call-done), kind=kOutput, calls=%fused_computation.51 | convolution fusion | flops 14495514624 | bytes 40894464 | tf_op jit(solution)/shard_map/dot_general | solution.py:83
  381.8 27.0 %reduce-scatter.9.cloned.1.call-done = f32[768,128]{1,0:T(8,128)} async-done(((f32[3072,128]{1,0:T(8,128)}), f32[768,128]{1,0:T(8,128)}) %reduce-scatter.9.cloned.1.call-update) | async-done | bytes 393232 | tf_op jit(solution)/shard_map/reduce_scatter | solution.py:101
  408.9 21.2 %all-gather.15.cloned.1.call-done = f32[3072,128]{1,0:T(8,128)} async-done(((f32[768,128]{1,0:T(8,128)}), f32[3072,128]{1,0:T(8,128)}) %all-gather.15.cloned.1.call-update) | async-done | bytes 1572880 | tf_op jit(solution)/shard_map/all_gather | solution.py:102
  430.1 64.0 %fusion.26 = f32[3072,128]{1,0:T(8,128)} fusion(f32[3072,3072]{1,0:T(8,128)} %fusion, f32[3072,128]{1,0:T(8,128)} %all-gather.15.cloned.1.call-done), kind=kOutput, calls=%fused_computation.52 | convolution fusion | flops 14495514624 | bytes 40894464 | tf_op jit(solution)/shard_map/dot_general | solution.py:91
  494.1 35.6 %reduce-scatter.11.cloned.1.call-done = f32[768,128]{1,0:T(8,128)} async-done(((f32[3072,128]{1,0:T(8,128)}), f32[768,128]{1,0:T(8,128)}) %reduce-scatter.11.cloned.1.call-update) | async-done | bytes 393232 | tf_op jit(solution)/shard_map/reduce_scatter | solution.py:103
  529.7 1.8 multiply_subtract_fusion
  (44 shorter events, 2.3 us)
Async XLA Ops:
  6.5 77.1 %copy-start = (f32[768,256]{1,0:T(8,128)S(1)}, f32[768,256]{1,0:T(8,128)}, u32[]{:S(2)}) copy-start(f32[768,256]{1,0:T(8,128)} %param.5) | copy-start | bytes 2359300
  6.5 78.1 %all-gather.7.cloned.1.call-start = ((), (), s32[]{:S(2)}) async-start(), calls=%async_computation.4 | async-start | bytes 3932160 | tf_op jit(solution)/shard_map/all_gather | solution.py:44
  11.7 112.8 %all-gather.9.cloned.1.call-start = ((), (), s32[]{:S(2)}) async-start(), calls=%async_computation.5 | async-start | bytes 1966080 | tf_op jit(solution)/shard_map/all_gather | solution.py:100
  11.7 22.9 %collective-permute-start = (f32[768,256]{1,0:T(8,128)}, f32[768,256]{1,0:T(8,128)S(1)}, u32[]{:S(2)}, u32[]{:S(2)}) collective-permute-start(f32[768,256]{1,0:T(8,128)} %subtract_multiply_fusion), channel_id=1, source_target_pairs={{0,4},{4,8},{8,12},{12,0},{1,5},{5,9},{9,13},{13,1},{2,6},{6,10},{... | collective-permute-start | bytes 2359304 | tf_op jit(solution)/shard_map/ppermute | solution.py:18
  34.6 20.5 %collective-permute-start.1 = (f32[768,256]{1,0:T(8,128)S(1)}, f32[768,256]{1,0:T(8,128)S(1)}, u32[]{:S(2)}, u32[]{:S(2)}) collective-permute-start(f32[768,256]{1,0:T(8,128)S(1)} %collective-permute-done), channel_id=1, source_target_pairs={{0,4},{4,8},{8,12},{12,0},{1,5},{5,9},{9,13},{13,1},{2,6},{6,10},{... | collective-permute-start | bytes 2359304 | tf_op jit(solution)/shard_map/ppermute | solution.py:18
  55.1 28.3 %collective-permute-start.2 = (f32[768,256]{1,0:T(8,128)S(1)}, f32[768,256]{1,0:T(8,128)S(1)}, u32[]{:S(2)}, u32[]{:S(2)}) collective-permute-start(f32[768,256]{1,0:T(8,128)S(1)} %collective-permute-done.1), channel_id=1, source_target_pairs={{0,4},{4,8},{8,12},{12,0},{1,5},{5,9},{9,13},{13,1},{2,6},{6,10},{... | collective-permute-start | bytes 2359304 | tf_op jit(solution)/shard_map/ppermute | solution.py:18
  55.1 132.8 %reduce-scatter.5.cloned.1.call-start = ((), (), s32[]{:S(2)}) async-start(), calls=%async_computation.6 | async-start | bytes 1966080 | tf_op jit(solution)/shard_map/reduce_scatter | solution.py:101
  159.4 49.6 %all-gather.11.cloned.1.call-start = ((), (), s32[]{:S(2)}) async-start(), calls=%async_computation.7 | async-start | bytes 1966080 | tf_op jit(solution)/shard_map/all_gather | solution.py:102
  188.0 85.7 %copy-start.3 = (f32[16]{0:T(128)S(1)}, f32[16]{0:T(128)}, u32[]{:S(2)}) copy-start(f32[16]{0:T(128)} %param.8) | copy-start | bytes 196
  188.0 121.2 %copy-start.1 = (f32[768,128]{1,0:T(8,128)S(1)}, f32[768,128]{1,0:T(8,128)}, u32[]{:S(2)}) copy-start(f32[768,128]{1,0:T(8,128)} %param.6) | copy-start | bytes 1179652
  188.0 121.2 %reduce-scatter.7.cloned.1.call-start = ((), (), s32[]{:S(2)}) async-start(), calls=%async_computation.8 | async-start | bytes 1966080 | tf_op jit(solution)/shard_map/reduce_scatter | solution.py:103
  273.6 73.4 %all-gather.13.cloned.1.call-start = ((), (), s32[]{:S(2)}) async-start(), calls=%async_computation.9 | async-start | bytes 1966080 | tf_op jit(solution)/shard_map/all_gather | solution.py:100
  311.0 97.8 %reduce-scatter.9.cloned.1.call-start = ((), (), s32[]{:S(2)}) async-start(), calls=%async_computation.10 | async-start | bytes 1966080 | tf_op jit(solution)/shard_map/reduce_scatter | solution.py:101
  381.8 48.3 %all-gather.15.cloned.1.call-start = ((), (), s32[]{:S(2)}) async-start(), calls=%async_computation.11 | async-start | bytes 1966080 | tf_op jit(solution)/shard_map/all_gather | solution.py:102
  408.9 120.8 %copy-start.2 = (f32[768,128]{1,0:T(8,128)S(1)}, f32[768,128]{1,0:T(8,128)}, u32[]{:S(2)}) copy-start(f32[768,128]{1,0:T(8,128)} %reduce-scatter.7.cloned.1.call-done) | copy-start | bytes 1179652
  408.9 120.8 %reduce-scatter.11.cloned.1.call-start = ((), (), s32[]{:S(2)}) async-start(), calls=%async_computation.12 | async-start | bytes 1966080 | tf_op jit(solution)/shard_map/reduce_scatter | solution.py:103
Sparse Core Ops, SparseCore 0:
  11.8 31.2 all-gather.6
  55.3 45.2 all-gather.8
  159.6 28.3 reduce-scatter.4
  189.4 19.6 all-gather.10
  273.7 35.4 reduce-scatter.6
  311.1 35.8 all-gather.12
  381.9 26.8 reduce-scatter.8
  410.4 19.6 all-gather.14
  494.2 35.4 reduce-scatter.10
